TPU v7x, 32 devices: a whole 2x2x4 slice. The times are simulated.
32 devices in a mesh: section: 16 (over z, y, core), dp: 2 (over x).
Axes of the slice: x: 2, y: 2, z: 4, core: 2. Of those that a mesh axis runs over, the one named last changes fastest.
Arguments:
- section_states: bfloat16 [16, 4, 2, 16, 16, 512], P('section', None, 'dp'), may hold values from -6 to 6
- conv_kernels: bfloat16 [16, 2, 1152, 512], P('section'), may hold values from -0.1875 to 0.1875
- top_feed: bfloat16 [3, 4, 2, 16, 16, 512], P(None, None, 'dp'), may hold values from -6 to 6
Outputs:
- final_states: bfloat16 [16, 4, 2, 16, 16, 512], P('section', None, 'dp')
- kernel_grads: float32 [16, 2, 1152, 512], P('section', None, 'dp')
All inputs are finite; a program needn't handle non-finite values.
Results may differ from a plain program's by a relative error of at most 0.024.
Values may be sent and summed in bfloat16 or wider, within the bound.
A program may use at most 128 MiB of HBM per device.

v0:
```python
import functools

import jax
import jax.numpy as jnp
from jax import lax
from jax.experimental import pallas as pl
from jax.experimental.pallas import tpu as pltpu
from jax.sharding import PartitionSpec as P

GW = 128
MESH = pl.DeviceIdType.MESH


def smooth_grad(value):
    sigma = jax.nn.sigmoid(value)
    return sigma * (1.0 + value * (1.0 - sigma))


def steps_in_order(groups, ticks):
    tuned = ((0, 0), (1, 0), (0, 1), (2, 0), (0, 2), (1, 1), (0, 3), (2, 1), (1, 2), (3, 0), (1, 3), (2, 2), (3, 1), (2, 3), (3, 2), (3, 3))
    if sorted(tuned) == [(group, tick) for group in range(groups) for tick in range(ticks)]:
        return tuned
    return [(group, tick) for tick in range(ticks) for group in range(groups)]


def fused_kernel(
    dims,
    states_ref,
    kernels_ref,
    feed_ref,
    final_ref,
    grads_ref,
    inbuf,
    outbuf,
    weights,
    flipped,
    taps,
    acc,
    gsend,
    gown,
    grecv,
    in_sem,
    send_sem,
    weight_sem,
    gsend_sem,
    grecv_sem,
):
    ticks, groups, images, height, width, share, shards = dims
    cells = height * width
    order = steps_in_order(groups, ticks)
    sends = ((1, 2), (0, 1), (3, 1))
    rows = images * cells
    pad = (height + 2) * width
    me = lax.axis_index("section")
    count = lax.axis_size("section")
    mine = lax.axis_index("dp")
    is_top = me == count - 1
    has_below = me > 0

    def lanes(group):
        start = group * GW
        return pl.ds(start if isinstance(group, int) else pl.multiple_of(start, GW), GW)

    def first_copy(group, stream):
        return pltpu.make_async_copy(
            states_ref.at[stream, :, lanes(group)],
            inbuf.at[0, group, stream],
            in_sem.at[0, group, stream],
        )

    def feed_copy(tick, group, stream):
        return pltpu.make_async_copy(
            feed_ref.at[tick - 1, stream, :, lanes(group)],
            inbuf.at[tick, group, stream],
            in_sem.at[tick, group, stream],
        )

    def weight_copy(group, branch):
        return pltpu.make_async_copy(
            kernels_ref.at[branch, :, lanes(group)],
            weights.at[branch, group],
            weight_sem.at[branch, group],
        )

    def below_copy(tick, group, stream, size):
        return pltpu.make_async_remote_copy(
            src_ref=outbuf.at[tick, group, pl.ds(stream, size)],
            dst_ref=inbuf.at[tick + 1, group, pl.ds(stream, size)],
            send_sem=send_sem.at[tick, group, stream],
            recv_sem=in_sem.at[tick + 1, group, stream],
            device_id={"section": me - 1},
            device_id_type=MESH,
        )

    def share_copy(group, branch, offset):
        partner = lax.rem(mine + offset, shards)
        return pltpu.make_async_remote_copy(
            src_ref=gsend.at[branch, group, pl.ds(pl.multiple_of(partner * share, 16), share)],
            dst_ref=grecv.at[offset - 1, branch, group],
            send_sem=gsend_sem.at[offset - 1, branch, group],
            recv_sem=grecv_sem.at[offset - 1, branch, group],
            device_id={"dp": partner},
            device_id_type=MESH,
        )

    for group in range(groups):
        for stream in range(4):
            first_copy(group, stream).start()
        for branch in range(2):
            weight_copy(group, branch).start()

    @pl.when(is_top)
    def _():
        @pl.loop(1, ticks)
        def _(tick):
            for group in range(groups):
                for stream in range(4):
                    feed_copy(tick, group, stream).start()

    barrier = pltpu.get_barrier_semaphore()

    @pl.when(has_below)
    def _():
        pl.semaphore_signal(barrier, inc=1, device_id={"section": me - 1}, device_id_type=MESH)

    @pl.when(jnp.logical_not(is_top))
    def _():
        pl.semaphore_signal(barrier, inc=1, device_id={"section": me + 1}, device_id_type=MESH)

    for offset in range(1, shards):
        pl.semaphore_signal(
            barrier,
            inc=1,
            device_id={"dp": lax.rem(mine + offset, shards)},
            device_id_type=MESH,
        )

    edge = jnp.zeros((4, images, width, 3 * GW), jnp.bfloat16)
    taps[:, :, 0:width, :] = edge
    taps[:, :, pad - width : pad, :] = edge
    acc[...] = jnp.zeros_like(acc)

    greeted = jnp.where(has_below, 1, 0) + jnp.where(is_top, 0, 1) + (shards - 1)
    column = lax.rem(lax.broadcasted_iota(jnp.int32, (rows, GW), 0), width)
    at_left = column == 0
    at_right = column == width - 1

    def put_taps(slot, wide):
        left = jnp.where(at_left, 0.0, pltpu.roll(wide, 1, 0))
        right = jnp.where(at_right, 0.0, pltpu.roll(wide, rows - 1, 0))
        for place, piece in enumerate((left, wide, right)):
            taps[slot, :, width : width + cells, place * GW : (place + 1) * GW] = piece.astype(
                jnp.bfloat16
            ).reshape(images, cells, GW)

    def slab(slot):
        return jnp.concatenate(
            [
                taps[slot, :, row * width : row * width + cells, :].reshape(rows, 3 * GW)
                for row in range(3)
            ],
            axis=1,
        )

    def conv(slot, branch, group):
        return lax.dot_general(
            slab(slot),
            weights[branch, group],
            (((1,), (0,)), ((), ())),
            preferred_element_type=jnp.float32,
        )

    def conv_t(slot, branch, group):
        return lax.dot_general(
            slab(slot),
            flipped[branch, group],
            (((1,), (0,)), ((), ())),
            preferred_element_type=jnp.float32,
        )

    def add_term(branch, group, slot, grad):
        acc[branch, group] += lax.dot_general(
            grad,
            slab(slot),
            (((0,), (0,)), ((), ())),
            preferred_element_type=jnp.float32,
        )

    @pl.loop(0, ticks * groups)
    def _(step):
        word = jnp.int32(0)
        for place in range(0, len(order), 3):
            packed = 0
            for at, (at_group, at_tick) in enumerate(order[place : place + 3]):
                packed |= (at_group * 32 + at_tick) << (10 * at)
            word = jnp.where(step >= place, packed, word)
        entry = lax.shift_right_logical(word, 10 * lax.rem(step, 3))
        tick = entry & 31
        group = lax.shift_right_logical(entry, 5) & 31

        @pl.when(tick == 0)
        def _():
            for stream in range(4):
                first_copy(group, stream).wait()
            for branch in range(2):
                weight_copy(group, branch).wait()
                for k in range(9):
                    flipped[branch, group, k * GW : (k + 1) * GW, :] = weights[
                        branch, group, (8 - k) * GW : (9 - k) * GW, :
                    ].T

        @pl.when(jnp.logical_and(tick > 0, is_top))
        def _():
            for stream in range(4):
                feed_copy(tick, group, stream).wait()

        @pl.when(jnp.logical_and(tick > 0, jnp.logical_not(is_top)))
        def _():
            for stream, size in sends:
                below_copy(tick - 1, group, stream, size).wait_recv()

        def give(first, size):
            @pl.when(jnp.logical_and(tick < ticks - 1, has_below))
            def _():
                below_copy(tick, group, first, size).start()

            @pl.when(tick == ticks - 1)
            def _():
                for stream in range(first, first + size):
                    final_ref[stream, :, lanes(group)] = outbuf[tick, group, stream]

        def hand_on(branch):
            @pl.when(tick == ticks - 1)
            def _():
                for k in range(9):
                    block = acc[branch, group, :, k * GW : (k + 1) * GW].T * (1.0 / cells)
                    gown[branch, group, k * GW : (k + 1) * GW, :] = block
                    gsend[branch, group, k * GW : (k + 1) * GW, :] = block.astype(jnp.bfloat16)
                for offset in range(1, shards):
                    share_copy(group, branch, offset).start()

        one = inbuf[tick, group, 0].astype(jnp.float32)
        grad_two = inbuf[tick, group, 3]
        put_taps(0, jax.nn.silu(one).astype(jnp.bfloat16).astype(jnp.float32))
        put_taps(1, grad_two.astype(jnp.float32))
        two = inbuf[tick, group, 1].astype(jnp.float32)
        input_two = (two - conv(0, 1, group)).astype(jnp.bfloat16)
        outbuf[tick, group, 1] = input_two
        put_taps(2, jax.nn.silu(input_two.astype(jnp.float32)).astype(jnp.bfloat16).astype(jnp.float32))
        total_one = (
            inbuf[tick, group, 2].astype(jnp.float32) + conv_t(1, 1, group) * smooth_grad(one)
        ).astype(jnp.bfloat16)
        outbuf[tick, group, 2] = total_one
        put_taps(3, total_one.astype(jnp.float32))
        add_term(1, group, 0, inbuf[tick, group, 3])

        @pl.when(step == 0)
        def _():
            pl.semaphore_wait(barrier, greeted)

        give(1, 2)
        hand_on(1)
        outbuf[tick, group, 0] = (
            inbuf[tick, group, 0].astype(jnp.float32) - conv(2, 0, group)
        ).astype(jnp.bfloat16)
        outbuf[tick, group, 3] = (
            inbuf[tick, group, 3].astype(jnp.float32)
            + conv_t(3, 0, group) * smooth_grad(outbuf[tick, group, 1].astype(jnp.float32))
        ).astype(jnp.bfloat16)
        give(0, 1)
        give(3, 1)
        add_term(0, group, 2, outbuf[tick, group, 2])
        hand_on(0)

    @pl.loop(0, groups)
    def _(group):
        for branch in (1, 0):
            total = gown[branch, group, pl.ds(pl.multiple_of(mine * share, 16), share), :]
            for offset in range(1, shards):
                share_copy(group, branch, offset).wait_recv()
                total = total + grecv[offset - 1, branch, group].astype(jnp.float32)
            grads_ref[branch, :, lanes(group)] = total

    @pl.loop(0, groups)
    def _(group):
        for branch in range(2):
            for offset in range(1, shards):
                share_copy(group, branch, offset).wait_send()
        @pl.when(has_below)
        def _():
            for tick in range(ticks - 1):
                for stream, size in sends:
                    below_copy(tick, group, stream, size).wait_send()


def on_device(section_states, conv_kernels, top_feed):
    _, _, images, height, width, chans = section_states.shape
    ticks = top_feed.shape[0] + 1
    groups = chans // GW
    shards = lax.axis_size("dp")
    taps_rows = conv_kernels.shape[2]
    share = taps_rows // shards
    rows = images * height * width
    states = section_states.reshape(4, rows, chans)
    feed = top_feed.reshape(ticks - 1, 4, rows, chans)
    dims = (ticks, groups, images, height, width, share, shards)
    anywhere = pl.BlockSpec(memory_space=pltpu.HBM)
    dma = pltpu.SemaphoreType.DMA
    final, grads = pl.pallas_call(
        functools.partial(fused_kernel, dims),
        out_shape=(
            pltpu.VMEM((4, rows, chans), jnp.bfloat16),
            pltpu.VMEM((2, share, chans), jnp.float32),
        ),
        in_specs=[anywhere] * 3,
        out_specs=[pl.BlockSpec(memory_space=pltpu.VMEM)] * 2,
        scratch_shapes=[
            pltpu.VMEM((ticks, groups, 4, rows, GW), jnp.bfloat16),
            pltpu.VMEM((ticks, groups, 4, rows, GW), jnp.bfloat16),
            pltpu.VMEM((2, groups, taps_rows, GW), jnp.bfloat16),
            pltpu.VMEM((2, groups, taps_rows, GW), jnp.bfloat16),
            pltpu.VMEM((4, images, (height + 2) * width, 3 * GW), jnp.bfloat16),
            pltpu.VMEM((2, groups, GW, taps_rows), jnp.float32),
            pltpu.VMEM((2, groups, taps_rows, GW), jnp.bfloat16),
            pltpu.VMEM((2, groups, taps_rows, GW), jnp.float32),
            pltpu.VMEM((max(shards - 1, 1), 2, groups, share, GW), jnp.bfloat16),
            dma((ticks, groups, 4)),
            dma((ticks, groups, 4)),
            dma((2, groups)),
            dma((max(shards - 1, 1), 2, groups)),
            dma((max(shards - 1, 1), 2, groups)),
        ],
        compiler_params=pltpu.CompilerParams(
            collective_id=0, has_side_effects=True, vmem_limit_bytes=56 * 1024 * 1024
        ),
    )(states, conv_kernels[0], feed)
    return (
        final.reshape(section_states.shape),
        grads.reshape(1, 2, share, chans),
    )


def solution(mesh):
    return jax.shard_map(
        on_device,
        mesh=mesh,
        in_specs=(
            P("section", None, "dp", None, None, None),
            P("section", None, None, None),
            P(None, None, "dp", None, None, None),
        ),
        out_specs=(P("section", None, "dp", None, None, None), P("section", None, "dp", None)),
        check_vma=False,
    )
```

profile of v0, /device:TPU:0, one launch (start us, length us, event | category | flops | bytes accessed | tf_op | source)
XLA Modules:
  0.0 53.6 jit_solution(2610412273734577233)
XLA Ops:
  0.6 50.6 %shard_map.50 = (bf16[4,256,512]{2,1,0:T(8,128)(2,1)S(1)}, f32[2,576,512]{2,1,0:T(8,128)S(1)}) custom-call(bf16[4,256,512]{2,1,0:T(8,128)(2,1)} %bitcast.11, bf16[2,1152,512]{2,1,0:T(8,128)(2,1)} %bitcast.10, bf16[3,4,256,512]{3,2,1,0:T(8,128)(2,1)} %bitcast.9), custom_call_target="tpu_custom_call" | custom-call | tf_op jit(solution)/shard_map/pallas_call | solution.py:309
  51.2 1.0 %copy.8 = bf16[1,4,1,16,16,512]{5,4,3,2,1,0:T(8,128)(2,1)} copy(bf16[1,4,1,16,16,512]{5,4,3,2,1,0:T(8,128)(2,1)S(1)} %bitcast.8) | data formatting | bytes 2097152
  52.2 1.4 %copy.9 = f32[1,2,576,512]{3,2,1,0:T(8,128)} copy(f32[1,2,576,512]{3,2,1,0:T(8,128)S(1)} %bitcast.7) | data formatting | bytes 4718592
where the time goes:
time: 53.8 us; the launch traced here: 53.6 us
  Pallas kernels  50.6 us (94%)
  local copies, waits for them, and re-layouts  2.38 us (4%)
  between operations  0.64 us (1%)
    pallas_call x1, Pallas kernels, on_device(): pl.pallas_call(functools.partial(fused_kernel, dims), out_shape=(pltpu.VM...  50.6 us
    unnamed x2, local copies, waits for them, and re-layouts  2.38 us

commit v1 on v0

v1 whole, which is shorter than its diff:
```python
import functools

import jax
import jax.numpy as jnp
from jax import lax
from jax.experimental import pallas as pl
from jax.experimental.pallas import tpu as pltpu
from jax.sharding import PartitionSpec as P

GW = 128
MESH = pl.DeviceIdType.MESH
PARTS = ((0, 1, 0), (3, 1, 0), (1, 2, 1))


def smooth_grad(value):
    sigma = jax.nn.sigmoid(value)
    return sigma * (1.0 + value * (1.0 - sigma))


def steps_in_order(groups, ticks):
    tuned = ((0, 0), (1, 0), (0, 1), (2, 0), (0, 2), (1, 1), (0, 3), (2, 1), (1, 2), (3, 0), (1, 3), (2, 2), (3, 1), (2, 3), (3, 2), (3, 3))
    if sorted(tuned) == [(group, tick) for group in range(groups) for tick in range(ticks)]:
        return tuned
    return [(group, tick) for tick in range(ticks) for group in range(groups)]


def fused_kernel(
    dims,
    states_ref,
    kernels_ref,
    feed_ref,
    final_ref,
    grads_ref,
    inbuf,
    outbuf,
    weights,
    flipped,
    padded,
    acc,
    gsend,
    gown,
    grecv,
    in_sem,
    send_sem,
    weight_sem,
    gsend_sem,
    grecv_sem,
):
    ticks, groups, images, height, width, share, shards = dims
    cells = height * width
    order = steps_in_order(groups, ticks)
    rows = images * cells
    pad = (height + 2) * width
    me = lax.axis_index("section")
    count = lax.axis_size("section")
    mine = lax.axis_index("dp")
    is_top = me == count - 1
    has_below = me > 0

    def lanes(group):
        start = group * GW
        return pl.ds(start if isinstance(group, int) else pl.multiple_of(start, GW), GW)

    def first_copy(group):
        return pltpu.make_async_copy(
            states_ref.at[:, :, lanes(group)], inbuf.at[0, group], in_sem.at[0, group, 0]
        )

    def feed_copies(tick, group):
        for first, size, part in PARTS:
            yield pltpu.make_async_copy(
                feed_ref.at[tick - 1, pl.ds(first, size), :, lanes(group)],
                inbuf.at[tick, group, pl.ds(first, size)],
                in_sem.at[tick, group, part],
            )

    def weight_copy(group, branch, column):
        return pltpu.make_async_copy(
            kernels_ref.at[branch, :, column, :, lanes(group)],
            weights.at[branch, group, :, :, pl.ds(column * GW, GW)],
            weight_sem.at[branch, group, column],
        )

    def below_copies(tick, group, wanted):
        for first, size, part in PARTS:
            if part == wanted:
                yield pltpu.make_async_remote_copy(
                    src_ref=outbuf.at[tick, group, pl.ds(first, size)],
                    dst_ref=inbuf.at[tick + 1, group, pl.ds(first, size)],
                    send_sem=send_sem.at[part],
                    recv_sem=in_sem.at[tick + 1, group, part],
                    device_id={"section": me - 1},
                    device_id_type=MESH,
                )

    def arrived(tick, group, part):
        pair = inbuf.at[tick, group, pl.ds(1, 2)]
        pltpu.make_async_copy(pair, pair, in_sem.at[tick, group, part]).wait()

    def share_copy(group, branch, offset):
        partner = lax.rem(mine + offset, shards)
        return pltpu.make_async_remote_copy(
            src_ref=gsend.at[branch, group, pl.ds(pl.multiple_of(partner * share, 16), share)],
            dst_ref=grecv.at[offset - 1, branch, group],
            send_sem=gsend_sem.at[offset - 1],
            recv_sem=grecv_sem.at[offset - 1, branch, group],
            device_id={"dp": partner},
            device_id_type=MESH,
        )

    barrier = pltpu.get_barrier_semaphore()

    @pl.when(has_below)
    def _():
        pl.semaphore_signal(barrier, inc=1, device_id={"section": me - 1}, device_id_type=MESH)

    @pl.when(jnp.logical_not(is_top))
    def _():
        pl.semaphore_signal(barrier, inc=1, device_id={"section": me + 1}, device_id_type=MESH)

    for offset in range(1, shards):
        pl.semaphore_signal(
            barrier,
            inc=1,
            device_id={"dp": lax.rem(mine + offset, shards)},
            device_id_type=MESH,
        )

    for group in range(groups):
        first_copy(group).start()
        for branch in (1, 0):
            for column in range(3):
                weight_copy(group, branch, column).start()

    @pl.when(is_top)
    def _():
        @pl.loop(1, ticks)
        def _(tick):
            for group in range(groups):
                for copy in feed_copies(tick, group):
                    copy.start()

    edge = jnp.zeros((4, images, width, GW), jnp.bfloat16)
    padded[:, :, 0:width, :] = edge
    padded[:, :, pad - width : pad, :] = edge

    greeted = jnp.where(has_below, 1, 0) + jnp.where(is_top, 0, 1) + (shards - 1)
    column = lax.rem(lax.broadcasted_iota(jnp.int32, (rows, GW), 0), width)
    at_left = column == 0
    at_right = column == width - 1
    chunk = GW if rows % GW == 0 and GW % width == 0 else rows
    lane_column = lax.rem(lax.broadcasted_iota(jnp.int32, (GW, chunk), 1), width)
    lane_left = lane_column == 0
    lane_right = lane_column == width - 1

    def put(slot, field):
        padded[slot, :, width : width + cells, :] = field.reshape(images, cells, GW)

    def slab(slot, order):
        return jnp.concatenate(
            [
                padded[slot, :, row * width : row * width + cells, :].reshape(rows, GW)
                for row in order
            ],
            axis=1,
        )

    def mix(slot, kernel):
        wide = lax.dot_general(
            slab(slot, (0, 1, 2)),
            kernel.reshape(3 * GW, 3 * GW),
            (((1,), (0,)), ((), ())),
            preferred_element_type=jnp.float32,
        )
        left = jnp.where(at_left, 0.0, pltpu.roll(wide[:, :GW], 1, 0))
        right = jnp.where(at_right, 0.0, pltpu.roll(wide[:, 2 * GW :], rows - 1, 0))
        return wide[:, GW : 2 * GW] + left + right

    def turned(field):
        flat = field.T
        parts = ([], [], [])
        for start in range(0, rows, chunk):
            piece = flat[:, start : start + chunk].astype(jnp.float32)
            left = jnp.where(lane_left, 0.0, pltpu.roll(piece, 1, 1))
            right = jnp.where(lane_right, 0.0, pltpu.roll(piece, chunk - 1, 1))
            parts[0].append(left.astype(jnp.bfloat16))
            parts[1].append(flat[:, start : start + chunk])
            parts[2].append(right.astype(jnp.bfloat16))
        return jnp.concatenate([jnp.concatenate(part, axis=1) for part in parts], axis=0)

    def add_term(branch, group, field, slot):
        acc[branch, group] += lax.dot_general(
            turned(field),
            slab(slot, (2, 1, 0)),
            (((1,), (0,)), ((), ())),
            preferred_element_type=jnp.float32,
        )

    def hand_on(branch, group):
        for k in range(9):
            down, side = divmod(k, 3)
            block = acc[
                branch, group, side * GW : (side + 1) * GW, down * GW : (down + 1) * GW
            ] * (1.0 / cells)
            gown[branch, group, k * GW : (k + 1) * GW, :] = block
            gsend[branch, group, k * GW : (k + 1) * GW, :] = block.astype(jnp.bfloat16)
        for offset in range(1, shards):
            share_copy(group, branch, offset).start()

    def prepare(branch, group):
        for column in range(3):
            weight_copy(group, branch, column).wait()
        for down in range(3):
            for side in range(3):
                flipped[branch, group, down, :, side * GW : (side + 1) * GW] = weights[
                    branch, group, 2 - down, :, (2 - side) * GW : (3 - side) * GW
                ].T
        acc[branch, group] = jnp.zeros((3 * GW, 3 * GW), jnp.float32)

    @pl.loop(0, ticks * groups)
    def _(step):
        word = jnp.int32(0)
        for place in range(0, len(order), 3):
            packed = 0
            for at, (at_group, at_tick) in enumerate(order[place : place + 3]):
                packed |= (at_group * 32 + at_tick) << (10 * at)
            word = jnp.where(step >= place, packed, word)
        entry = lax.shift_right_logical(word, 10 * lax.rem(step, 3))
        tick = entry & 31
        group = lax.shift_right_logical(entry, 5) & 31
        is_first = tick == 0
        is_last = tick == ticks - 1
        sending = jnp.logical_and(jnp.logical_not(is_last), has_below)

        def give(part):
            for copy in below_copies(tick, group, part):
                copy.start()

        def finish(streams):
            for stream in streams:
                final_ref[stream, :, lanes(group)] = outbuf[tick, group, stream]

        @pl.when(is_first)
        def _():
            first_copy(group).wait()
            prepare(1, group)

        @pl.when(jnp.logical_not(is_first))
        def _():
            arrived(tick, group, 0)

        one = inbuf[tick, group, 0].astype(jnp.float32)
        act_one = jax.nn.silu(one).astype(jnp.bfloat16)
        put(0, act_one)
        put(1, inbuf[tick, group, 3])
        add_term(1, group, act_one, 1)
        mixed_one = mix(0, weights[1, group])
        mixed_two = mix(1, flipped[1, group]) * smooth_grad(one)

        @pl.when(step == 0)
        def _():
            pl.semaphore_wait(barrier, greeted)

        @pl.when(is_last)
        def _():
            hand_on(1, group)

        @pl.when(jnp.logical_not(is_first))
        def _():
            arrived(tick, group, 1)

        input_two = (inbuf[tick, group, 1].astype(jnp.float32) - mixed_one).astype(jnp.bfloat16)
        outbuf[tick, group, 1] = input_two
        total_one = (inbuf[tick, group, 2].astype(jnp.float32) + mixed_two).astype(jnp.bfloat16)
        outbuf[tick, group, 2] = total_one

        @pl.when(is_first)
        def _():
            @pl.when(sending)
            def _():
                give(1)

            prepare(0, group)

        wide_two = input_two.astype(jnp.float32)
        act_two = jax.nn.silu(wide_two).astype(jnp.bfloat16)
        put(2, act_two)
        put(3, total_one)
        outbuf[tick, group, 0] = (
            inbuf[tick, group, 0].astype(jnp.float32) - mix(2, weights[0, group])
        ).astype(jnp.bfloat16)
        outbuf[tick, group, 3] = (
            inbuf[tick, group, 3].astype(jnp.float32)
            + mix(3, flipped[0, group]) * smooth_grad(wide_two)
        ).astype(jnp.bfloat16)

        @pl.when(sending)
        def _():
            give(0)

            @pl.when(jnp.logical_not(is_first))
            def _():
                give(1)

        add_term(0, group, act_two, 3)

        @pl.when(is_last)
        def _():
            hand_on(0, group)
            finish(range(4))

    @pl.loop(0, groups)
    def _(group):
        for branch in (1, 0):
            total = gown[branch, group, pl.ds(pl.multiple_of(mine * share, 16), share), :]
            for offset in range(1, shards):
                share_copy(group, branch, offset).wait_recv()
                total = total + grecv[offset - 1, branch, group].astype(jnp.float32)
            grads_ref[branch, :, lanes(group)] = total

    for offset in range(1, shards):
        every = gsend.at[:, :, pl.ds(0, share)]
        pltpu.make_async_copy(every, every, gsend_sem.at[offset - 1]).wait()

    @pl.when(has_below)
    def _():
        for part in range(2):
            every = outbuf.at[pl.ds(0, ticks - 1), :, pl.ds(0, 2)]
            pltpu.make_async_copy(every, every, send_sem.at[part]).wait()


def on_device(section_states, conv_kernels, top_feed):
    _, _, images, height, width, chans = section_states.shape
    ticks = top_feed.shape[0] + 1
    groups = chans // GW
    shards = lax.axis_size("dp")
    taps_rows = conv_kernels.shape[2]
    share = taps_rows // shards
    rows = images * height * width
    states = section_states.reshape(4, rows, chans)
    feed = top_feed.reshape(ticks - 1, 4, rows, chans)
    dims = (ticks, groups, images, height, width, share, shards)
    anywhere = pl.BlockSpec(memory_space=pltpu.HBM)
    dma = pltpu.SemaphoreType.DMA
    final, grads = pl.pallas_call(
        functools.partial(fused_kernel, dims),
        out_shape=(
            pltpu.VMEM((4, rows, chans), jnp.bfloat16),
            pltpu.VMEM((2, share, chans), jnp.float32),
        ),
        in_specs=[anywhere] * 3,
        out_specs=[pl.BlockSpec(memory_space=pltpu.VMEM)] * 2,
        scratch_shapes=[
            pltpu.VMEM((ticks, groups, 4, rows, GW), jnp.bfloat16),
            pltpu.VMEM((ticks, groups, 4, rows, GW), jnp.bfloat16),
            pltpu.VMEM((2, groups, 3, GW, 3 * GW), jnp.bfloat16),
            pltpu.VMEM((2, groups, 3, GW, 3 * GW), jnp.bfloat16),
            pltpu.VMEM((4, images, (height + 2) * width, GW), jnp.bfloat16),
            pltpu.VMEM((2, groups, 3 * GW, 3 * GW), jnp.float32),
            pltpu.VMEM((2, groups, taps_rows, GW), jnp.bfloat16),
            pltpu.VMEM((2, groups, taps_rows, GW), jnp.float32),
            pltpu.VMEM((max(shards - 1, 1), 2, groups, share, GW), jnp.bfloat16),
            dma((ticks, groups, 2)),
            dma((2,)),
            dma((2, groups, 3)),
            dma((max(shards - 1, 1),)),
            dma((max(shards - 1, 1), 2, groups)),
        ],
        compiler_params=pltpu.CompilerParams(
            collective_id=0, has_side_effects=True, vmem_limit_bytes=56 * 1024 * 1024
        ),
    )(states, conv_kernels.reshape(2, 3, 3, GW, chans), feed)
    return (
        final.reshape(section_states.shape),
        grads.reshape(1, 2, share, chans),
    )


def solution(mesh):
    return jax.shard_map(
        on_device,
        mesh=mesh,
        in_specs=(
            P("section", None, "dp", None, None, None),
            P("section", None, None, None),
            P(None, None, "dp", None, None, None),
        ),
        out_specs=(P("section", None, "dp", None, None, None), P("section", None, "dp", None)),
        check_vma=False,
    )
```

time: 53.8 us -> 52.3 us (0.972)
  Pallas kernels: 50.6 us -> 49.2 us
    pallas_call x1, Pallas kernels: 50.6 us -> 49.2 us  [on_device(): pl.pallas_call(functools.partial(fused_kernel, dims), out_shape=(pltpu.VM...]
where the time goes in v1:
time: 52.3 us; the launch traced here: 52.2 us
  Pallas kernels  49.2 us (94%)
  local copies, waits for them, and re-layouts  2.38 us (5%)
  between operations  0.64 us (1%)
    pallas_call x1, Pallas kernels, on_device(): pl.pallas_call(functools.partial(fused_kernel, dims), out_shape=(pltpu.VM...  49.2 us
    unnamed x2, local copies, waits for them, and re-layouts  2.38 us

profile of v1, /device:TPU:0, one launch (start us, length us, event | category | flops | bytes accessed | tf_op | source)
XLA Modules:
  0.0 52.2 jit_solution(7845832099558077307)
XLA Ops:
  0.6 49.2 %shard_map.50 = (bf16[4,256,512]{2,1,0:T(8,128)(2,1)S(1)}, f32[2,576,512]{2,1,0:T(8,128)S(1)}) custom-call(bf16[4,256,512]{2,1,0:T(8,128)(2,1)} %bitcast.11, bf16[2,3,3,128,512]{4,3,2,1,0:T(8,128)(2,1)} %bitcast.10, bf16[3,4,256,512]{3,2,1,0:T(8,128)(2,1)} %bitcast.9), custom_call_target="tpu_custom_call" | custom-call | tf_op jit(solution)/shard_map/pallas_call | solution.py:345
  49.8 1.0 %copy.8 = bf16[1,4,1,16,16,512]{5,4,3,2,1,0:T(8,128)(2,1)} copy(bf16[1,4,1,16,16,512]{5,4,3,2,1,0:T(8,128)(2,1)S(1)} %bitcast.8) | data formatting | bytes 2097152
  50.8 1.4 %copy.9 = f32[1,2,576,512]{3,2,1,0:T(8,128)} copy(f32[1,2,576,512]{3,2,1,0:T(8,128)S(1)} %bitcast.7) | data formatting | bytes 4718592

commit v2 on v1

--- a/solution.py
+++ b/solution.py
@@ -75,23 +75,26 @@
             )
 
     def weight_copy(group, branch, column):
+        row, place = ((0, 0), (0, 1), (3, 1))[column]
         return pltpu.make_async_copy(
             kernels_ref.at[branch, :, column, :, lanes(group)],
-            weights.at[branch, group, :, :, pl.ds(column * GW, GW)],
-            weight_sem.at[branch, group, column],
-        )
-
-    def below_copies(tick, group, wanted):
-        for first, size, part in PARTS:
-            if part == wanted:
-                yield pltpu.make_async_remote_copy(
-                    src_ref=outbuf.at[tick, group, pl.ds(first, size)],
-                    dst_ref=inbuf.at[tick + 1, group, pl.ds(first, size)],
-                    send_sem=send_sem.at[part],
-                    recv_sem=in_sem.at[tick + 1, group, part],
-                    device_id={"section": me - 1},
-                    device_id_type=MESH,
-                )
+            weights.at[branch, group, pl.ds(row, 3), :, pl.ds(place * GW, GW)],
+            weight_sem.at[branch, group],
+        )
+
+    def weights_arrived(group, branch):
+        whole = kernels_ref.at[branch, :, :, :, lanes(group)]
+        pltpu.make_async_copy(whole, whole, weight_sem.at[branch, group]).wait()
+
+    def below_copy(tick, group, first, size, part):
+        return pltpu.make_async_remote_copy(
+            src_ref=outbuf.at[tick, group, pl.ds(first, size)],
+            dst_ref=inbuf.at[tick + 1, group, pl.ds(first, size)],
+            send_sem=send_sem.at[part],
+            recv_sem=in_sem.at[tick + 1, group, part],
+            device_id={"section": me - 1},
+            device_id_type=MESH,
+        )
 
     def arrived(tick, group, part):
         pair = inbuf.at[tick, group, pl.ds(1, 2)]
@@ -140,9 +143,10 @@
                 for copy in feed_copies(tick, group):
                     copy.start()
 
-    edge = jnp.zeros((4, images, width, GW), jnp.bfloat16)
-    padded[:, :, 0:width, :] = edge
-    padded[:, :, pad - width : pad, :] = edge
+    edge = jnp.zeros((4, 2, images, width, GW), jnp.bfloat16)
+    padded[:, :, :, 0:width, :] = edge
+    padded[:, :, :, pad - width : pad, :] = edge
+    blank = jnp.zeros((3, GW, GW), jnp.bfloat16)
 
     greeted = jnp.where(has_below, 1, 0) + jnp.where(is_top, 0, 1) + (shards - 1)
     column = lax.rem(lax.broadcasted_iota(jnp.int32, (rows, GW), 0), width)
@@ -154,12 +158,16 @@
     lane_right = lane_column == width - 1
 
     def put(slot, field):
-        padded[slot, :, width : width + cells, :] = field.reshape(images, cells, GW)
-
-    def slab(slot, order):
+        wide = field.astype(jnp.float32)
+        ahead = jnp.where(at_right, 0.0, pltpu.roll(wide, rows - 1, 0)).astype(jnp.bfloat16)
+        for place, piece in enumerate((field, ahead)):
+            padded[slot, place, :, width : width + cells, :] = piece.reshape(images, cells, GW)
+
+    def slab(slot, places, order):
         return jnp.concatenate(
             [
-                padded[slot, :, row * width : row * width + cells, :].reshape(rows, GW)
+                padded[slot, place, :, row * width : row * width + cells, :].reshape(rows, GW)
+                for place in places
                 for row in order
             ],
             axis=1,
@@ -167,14 +175,12 @@
 
     def mix(slot, kernel):
         wide = lax.dot_general(
-            slab(slot, (0, 1, 2)),
-            kernel.reshape(3 * GW, 3 * GW),
+            slab(slot, (0, 1), (0, 1, 2)),
+            kernel.reshape(6 * GW, 2 * GW),
             (((1,), (0,)), ((), ())),
             preferred_element_type=jnp.float32,
         )
-        left = jnp.where(at_left, 0.0, pltpu.roll(wide[:, :GW], 1, 0))
-        right = jnp.where(at_right, 0.0, pltpu.roll(wide[:, 2 * GW :], rows - 1, 0))
-        return wide[:, GW : 2 * GW] + left + right
+        return wide[:, GW:] + jnp.where(at_left, 0.0, pltpu.roll(wide[:, :GW], 1, 0))
 
     def turned(field):
         flat = field.T
@@ -188,34 +194,106 @@
             parts[2].append(right.astype(jnp.bfloat16))
         return jnp.concatenate([jnp.concatenate(part, axis=1) for part in parts], axis=0)
 
-    def add_term(branch, group, field, slot):
-        acc[branch, group] += lax.dot_general(
+    def term_of(field, slot):
+        return lax.dot_general(
             turned(field),
-            slab(slot, (2, 1, 0)),
+            slab(slot, (0,), (2, 1, 0)),
             (((1,), (0,)), ((), ())),
             preferred_element_type=jnp.float32,
         )
 
-    def hand_on(branch, group):
+    def hand_on(branch, group, field, slot):
+        term = term_of(field, slot)
         for k in range(9):
             down, side = divmod(k, 3)
-            block = acc[
-                branch, group, side * GW : (side + 1) * GW, down * GW : (down + 1) * GW
-            ] * (1.0 / cells)
+            here = (
+                slice(side * GW, (side + 1) * GW),
+                slice(down * GW, (down + 1) * GW),
+            )
+            block = (acc[(branch, group, *here)] + term[here]) * (1.0 / cells)
             gown[branch, group, k * GW : (k + 1) * GW, :] = block
             gsend[branch, group, k * GW : (k + 1) * GW, :] = block.astype(jnp.bfloat16)
         for offset in range(1, shards):
             share_copy(group, branch, offset).start()
 
     def prepare(branch, group):
-        for column in range(3):
-            weight_copy(group, branch, column).wait()
+        weights[branch, group, 3:6, :, 0:GW] = blank
+        flipped[branch, group, 3:6, :, 0:GW] = blank
         for down in range(3):
-            for side in range(3):
-                flipped[branch, group, down, :, side * GW : (side + 1) * GW] = weights[
-                    branch, group, 2 - down, :, (2 - side) * GW : (3 - side) * GW
+            for side, (row, place) in enumerate(((0, 0), (0, 1), (3, 1))):
+                from_row, from_place = ((0, 0), (0, 1), (3, 1))[2 - side]
+                flipped[branch, group, row + down, :, place * GW : (place + 1) * GW] = weights[
+                    branch, group, from_row + 2 - down, :, from_place * GW : (from_place + 1) * GW
                 ].T
-        acc[branch, group] = jnp.zeros((3 * GW, 3 * GW), jnp.float32)
+
+    def section(step, tick, group, first, last):
+        def give(*copies):
+            @pl.when(has_below)
+            def _():
+                for copy in copies:
+                    below_copy(tick, group, *copy).start()
+
+        def keep(stream, value):
+            if last:
+                final_ref[stream, :, lanes(group)] = value
+            else:
+                outbuf[tick, group, stream] = value
+
+        def stream(at):
+            return inbuf[tick, group, at].astype(jnp.float32)
+
+        if first:
+            first_copy(group).wait()
+            weights_arrived(group, 1)
+        else:
+            arrived(tick, group, 0)
+        one = stream(0)
+        act_one = jax.nn.silu(one).astype(jnp.bfloat16)
+        put(0, act_one)
+        put(1, inbuf[tick, group, 3])
+        if last:
+            hand_on(1, group, act_one, 1)
+        mixed_one = mix(0, weights[1, group])
+        if first:
+            input_two = (stream(1) - mixed_one).astype(jnp.bfloat16)
+            keep(1, input_two)
+
+            @pl.when(step == 0)
+            def _():
+                pl.semaphore_wait(barrier, greeted)
+
+            give((1, 1, 1))
+            prepare(1, group)
+        mixed_two = mix(1, flipped[1, group]) * smooth_grad(one)
+        if not first:
+            arrived(tick, group, 1)
+            input_two = (stream(1) - mixed_one).astype(jnp.bfloat16)
+            keep(1, input_two)
+        total_one = (stream(2) + mixed_two).astype(jnp.bfloat16)
+        keep(2, total_one)
+        if first:
+            give((2, 1, 1))
+            weights_arrived(group, 0)
+            prepare(0, group)
+        wide_two = input_two.astype(jnp.float32)
+        act_two = jax.nn.silu(wide_two).astype(jnp.bfloat16)
+        put(2, act_two)
+        put(3, total_one)
+        if last:
+            hand_on(0, group, act_two, 3)
+        keep(0, (stream(0) - mix(2, weights[0, group])).astype(jnp.bfloat16))
+        keep(
+            3,
+            (stream(3) + mix(3, flipped[0, group]) * smooth_grad(wide_two)).astype(jnp.bfloat16),
+        )
+        if first:
+            give((0, 1, 0), (3, 1, 0))
+            acc[1, group] = term_of(act_one, 1)
+            acc[0, group] = term_of(act_two, 3)
+        elif not last:
+            give((0, 1, 0), (3, 1, 0), (1, 2, 1))
+            acc[1, group] += term_of(act_one, 1)
+            acc[0, group] += term_of(act_two, 3)
 
     @pl.loop(0, ticks * groups)
     def _(step):
@@ -228,86 +306,18 @@
         entry = lax.shift_right_logical(word, 10 * lax.rem(step, 3))
         tick = entry & 31
         group = lax.shift_right_logical(entry, 5) & 31
-        is_first = tick == 0
-        is_last = tick == ticks - 1
-        sending = jnp.logical_and(jnp.logical_not(is_last), has_below)
-
-        def give(part):
-            for copy in below_copies(tick, group, part):
-                copy.start()
-
-        def finish(streams):
-            for stream in streams:
-                final_ref[stream, :, lanes(group)] = outbuf[tick, group, stream]
-
-        @pl.when(is_first)
+
+        @pl.when(tick == 0)
         def _():
-            first_copy(group).wait()
-            prepare(1, group)
-
-        @pl.when(jnp.logical_not(is_first))
+            section(step, 0, group, True, False)
+
+        @pl.when(jnp.logical_and(tick > 0, tick < ticks - 1))
         def _():
-            arrived(tick, group, 0)
-
-        one = inbuf[tick, group, 0].astype(jnp.float32)
-        act_one = jax.nn.silu(one).astype(jnp.bfloat16)
-        put(0, act_one)
-        put(1, inbuf[tick, group, 3])
-        add_term(1, group, act_one, 1)
-        mixed_one = mix(0, weights[1, group])
-        mixed_two = mix(1, flipped[1, group]) * smooth_grad(one)
-
-        @pl.when(step == 0)
+            section(step, tick, group, False, False)
+
+        @pl.when(tick == ticks - 1)
         def _():
-            pl.semaphore_wait(barrier, greeted)
-
-        @pl.when(is_last)
-        def _():
-            hand_on(1, group)
-
-        @pl.when(jnp.logical_not(is_first))
-        def _():
-            arrived(tick, group, 1)
-
-        input_two = (inbuf[tick, group, 1].astype(jnp.float32) - mixed_one).astype(jnp.bfloat16)
-        outbuf[tick, group, 1] = input_two
-        total_one = (inbuf[tick, group, 2].astype(jnp.float32) + mixed_two).astype(jnp.bfloat16)
-        outbuf[tick, group, 2] = total_one
-
-        @pl.when(is_first)
-        def _():
-            @pl.when(sending)
-            def _():
-                give(1)
-
-            prepare(0, group)
-
-        wide_two = input_two.astype(jnp.float32)
-        act_two = jax.nn.silu(wide_two).astype(jnp.bfloat16)
-        put(2, act_two)
-        put(3, total_one)
-        outbuf[tick, group, 0] = (
-            inbuf[tick, group, 0].astype(jnp.float32) - mix(2, weights[0, group])
-        ).astype(jnp.bfloat16)
-        outbuf[tick, group, 3] = (
-            inbuf[tick, group, 3].astype(jnp.float32)
-            + mix(3, flipped[0, group]) * smooth_grad(wide_two)
-        ).astype(jnp.bfloat16)
-
-        @pl.when(sending)
-        def _():
-            give(0)
-
-            @pl.when(jnp.logical_not(is_first))
-            def _():
-                give(1)
-
-        add_term(0, group, act_two, 3)
-
-        @pl.when(is_last)
-        def _():
-            hand_on(0, group)
-            finish(range(4))
+            section(step, ticks - 1, group, False, True)
 
     @pl.loop(0, groups)
     def _(group):
@@ -327,6 +337,17 @@
         for part in range(2):
             every = outbuf.at[pl.ds(0, ticks - 1), :, pl.ds(0, 2)]
             pltpu.make_async_copy(every, every, send_sem.at[part]).wait()
+
+
+def write_kernel(final_ref, grads_ref, final_out, grads_out, sems):
+    copies = [
+        pltpu.make_async_copy(grads_ref, grads_out, sems.at[0]),
+        pltpu.make_async_copy(final_ref, final_out, sems.at[1]),
+    ]
+    for copy in copies:
+        copy.start()
+    for copy in copies:
+        copy.wait()
 
 
 def on_device(section_states, conv_kernels, top_feed):
@@ -353,16 +374,16 @@
         scratch_shapes=[
             pltpu.VMEM((ticks, groups, 4, rows, GW), jnp.bfloat16),
             pltpu.VMEM((ticks, groups, 4, rows, GW), jnp.bfloat16),
-            pltpu.VMEM((2, groups, 3, GW, 3 * GW), jnp.bfloat16),
-            pltpu.VMEM((2, groups, 3, GW, 3 * GW), jnp.bfloat16),
-            pltpu.VMEM((4, images, (height + 2) * width, GW), jnp.bfloat16),
+            pltpu.VMEM((2, groups, 6, GW, 2 * GW), jnp.bfloat16),
+            pltpu.VMEM((2, groups, 6, GW, 2 * GW), jnp.bfloat16),
+            pltpu.VMEM((4, 2, images, (height + 2) * width, GW), jnp.bfloat16),
             pltpu.VMEM((2, groups, 3 * GW, 3 * GW), jnp.float32),
             pltpu.VMEM((2, groups, taps_rows, GW), jnp.bfloat16),
             pltpu.VMEM((2, groups, taps_rows, GW), jnp.float32),
             pltpu.VMEM((max(shards - 1, 1), 2, groups, share, GW), jnp.bfloat16),
             dma((ticks, groups, 2)),
             dma((2,)),
-            dma((2, groups, 3)),
+            dma((2, groups)),
             dma((max(shards - 1, 1),)),
             dma((max(shards - 1, 1), 2, groups)),
         ],
@@ -370,6 +391,17 @@
             collective_id=0, has_side_effects=True, vmem_limit_bytes=56 * 1024 * 1024
         ),
     )(states, conv_kernels.reshape(2, 3, 3, GW, chans), feed)
+    final, grads = pl.pallas_call(
+        write_kernel,
+        out_shape=(
+            jax.ShapeDtypeStruct(final.shape, final.dtype),
+            jax.ShapeDtypeStruct(grads.shape, grads.dtype),
+        ),
+        in_specs=[pl.BlockSpec(memory_space=pltpu.VMEM)] * 2,
+        out_specs=[anywhere] * 2,
+        scratch_shapes=[dma((2,))],
+        compiler_params=pltpu.CompilerParams(vmem_limit_bytes=1024 * 1024),
+    )(final, grads)
     return (
         final.reshape(section_states.shape),
         grads.reshape(1, 2, share, chans),

time: 52.3 us -> 50.6 us (0.967)
  local copies, waits for them, and re-layouts: 2.38 us -> 0 us
  Pallas kernels: 49.2 us -> 49.8 us
    unnamed x2 -> x0, local copies, waits for them, and re-layouts: 2.38 us -> none
    pallas_call x0 -> x1, Pallas kernels: none -> 1.77 us  [on_device(): pl.pallas_call(write_kernel, out_shape=(jax.ShapeDtypeStruct(final.shape,...]
    pallas_call x1, Pallas kernels: 49.2 us -> 48 us  [on_device(): pl.pallas_call(functools.partial(fused_kernel, dims), out_shape=(pltpu.VM...]
where the time goes in v2:
time: 50.6 us; the launch traced here: 50.4 us
  Pallas kernels  49.8 us (98%)
  between operations  0.64 us (1%)
    pallas_call x1, Pallas kernels, on_device(): pl.pallas_call(functools.partial(fused_kernel, dims), out_shape=(pltpu.VM...  48 us
    pallas_call x1, Pallas kernels, on_device(): pl.pallas_call(write_kernel, out_shape=(jax.ShapeDtypeStruct(final.shape,...  1.77 us

profile of v2, /device:TPU:0, one launch (start us, length us, event | category | flops | bytes accessed | tf_op | source)
XLA Modules:
  0.0 50.4 jit_solution(1647360240617565693)
XLA Ops:
  0.6 48.0 %shard_map.50 = (bf16[4,256,512]{2,1,0:T(8,128)(2,1)S(1)}, f32[2,576,512]{2,1,0:T(8,128)S(1)}) custom-call(bf16[4,256,512]{2,1,0:T(8,128)(2,1)} %bitcast.9, bf16[2,3,3,128,512]{4,3,2,1,0:T(8,128)(2,1)} %bitcast.8, bf16[3,4,256,512]{3,2,1,0:T(8,128)(2,1)} %bitcast.7), custom_call_target="tpu_custom_call" | custom-call | tf_op jit(solution)/shard_map/pallas_call | solution.py:366
  48.6 1.8 %shard_map.51 = (bf16[4,256,512]{2,1,0:T(8,128)(2,1)}, f32[2,576,512]{2,1,0:T(8,128)}) custom-call(bf16[4,256,512]{2,1,0:T(8,128)(2,1)S(1)} %get-tuple-element.6.final_ref, f32[2,576,512]{2,1,0:T(8,128)S(1)} %get-tuple-element.7.grads_ref), custom_call_target="tpu_custom_call" | custom-call | tf_op jit(solution)/shard_map/pallas_call | solution.py:394

commit v3 on v2

--- a/solution.py
+++ b/solution.py
@@ -18,7 +18,7 @@
 
 
 def steps_in_order(groups, ticks):
-    tuned = ((0, 0), (1, 0), (0, 1), (2, 0), (0, 2), (1, 1), (0, 3), (2, 1), (1, 2), (3, 0), (1, 3), (2, 2), (3, 1), (2, 3), (3, 2), (3, 3))
+    tuned = ((0, 0), (0, 1), (1, 0), (0, 2), (1, 1), (0, 3), (2, 0), (1, 2), (2, 1), (1, 3), (3, 0), (2, 2), (3, 1), (2, 3), (3, 2), (3, 3))
     if sorted(tuned) == [(group, tick) for group in range(groups) for tick in range(ticks)]:
         return tuned
     return [(group, tick) for tick in range(ticks) for group in range(groups)]
@@ -43,6 +43,7 @@
     in_sem,
     send_sem,
     weight_sem,
+    turn_sem,
     gsend_sem,
     grecv_sem,
 ):
@@ -55,6 +56,8 @@
     count = lax.axis_size("section")
     mine = lax.axis_index("dp")
     is_top = me == count - 1
+    lower = jnp.logical_and(lax.rem(me, 2) == 0, me < count - 1)
+    upper = lax.rem(me, 2) == 1
     has_below = me > 0
 
     def lanes(group):
@@ -105,7 +108,7 @@
         return pltpu.make_async_remote_copy(
             src_ref=gsend.at[branch, group, pl.ds(pl.multiple_of(partner * share, 16), share)],
             dst_ref=grecv.at[offset - 1, branch, group],
-            send_sem=gsend_sem.at[offset - 1],
+            send_sem=gsend_sem.at[offset - 1, branch],
             recv_sem=grecv_sem.at[offset - 1, branch, group],
             device_id={"dp": partner},
             device_id_type=MESH,
@@ -213,8 +216,12 @@
             block = (acc[(branch, group, *here)] + term[here]) * (1.0 / cells)
             gown[branch, group, k * GW : (k + 1) * GW, :] = block
             gsend[branch, group, k * GW : (k + 1) * GW, :] = block.astype(jnp.bfloat16)
-        for offset in range(1, shards):
-            share_copy(group, branch, offset).start()
+        waiting = branch == 0 and shards > 1
+
+        @pl.when(jnp.logical_or(not waiting, jnp.logical_or(lax.rem(me, 2) == 0, group < groups - 1)))
+        def _():
+            for offset in range(1, shards):
+                share_copy(group, branch, offset).start()
 
     def prepare(branch, group):
         weights[branch, group, 3:6, :, 0:GW] = blank
@@ -319,6 +326,25 @@
         def _():
             section(step, ticks - 1, group, False, True)
 
+    def shared(branch):
+        for offset in range(1, shards):
+            every = gsend.at[branch, :, pl.ds(0, share)]
+            pltpu.make_async_copy(every, every, gsend_sem.at[offset - 1, branch]).wait()
+
+    if shards > 1:
+
+        @pl.when(upper)
+        def _():
+            pl.semaphore_wait(turn_sem, 1)
+            for offset in range(1, shards):
+                share_copy(groups - 1, 0, offset).start()
+
+        shared(1)
+
+        @pl.when(lower)
+        def _():
+            pl.semaphore_signal(turn_sem, inc=1, device_id={"section": me + 1}, device_id_type=MESH)
+
     @pl.loop(0, groups)
     def _(group):
         for branch in (1, 0):
@@ -328,9 +354,7 @@
                 total = total + grecv[offset - 1, branch, group].astype(jnp.float32)
             grads_ref[branch, :, lanes(group)] = total
 
-    for offset in range(1, shards):
-        every = gsend.at[:, :, pl.ds(0, share)]
-        pltpu.make_async_copy(every, every, gsend_sem.at[offset - 1]).wait()
+    shared(0)
 
     @pl.when(has_below)
     def _():
@@ -384,7 +408,8 @@
             dma((ticks, groups, 2)),
             dma((2,)),
             dma((2, groups)),
-            dma((max(shards - 1, 1),)),
+            pltpu.SemaphoreType.REGULAR,
+            dma((max(shards - 1, 1), 2)),
             dma((max(shards - 1, 1), 2, groups)),
         ],
         compiler_params=pltpu.CompilerParams(

time: 50.6 us -> 49.6 us (0.980)
  Pallas kernels: 49.8 us -> 48.6 us
    pallas_call x1, Pallas kernels: 48 us -> 46.8 us  [on_device(): pl.pallas_call(functools.partial(fused_kernel, dims), out_shape=(pltpu.VM...]
where the time goes in v3:
time: 49.6 us; the launch traced here: 49.2 us
  Pallas kernels  48.6 us (98%)
  between operations  0.64 us (1%)
    pallas_call x1, Pallas kernels, on_device(): pl.pallas_call(functools.partial(fused_kernel, dims), out_shape=(pltpu.VM...  46.8 us
    pallas_call x1, Pallas kernels, on_device(): pl.pallas_call(write_kernel, out_shape=(jax.ShapeDtypeStruct(final.shape,...  1.77 us

profile of v3, /device:TPU:0, one launch (start us, length us, event | category | flops | bytes accessed | tf_op | source)
XLA Modules:
  0.0 49.2 jit_solution(2779031100463406083)
XLA Ops:
  0.6 46.8 %shard_map.50 = (bf16[4,256,512]{2,1,0:T(8,128)(2,1)S(1)}, f32[2,576,512]{2,1,0:T(8,128)S(1)}) custom-call(bf16[4,256,512]{2,1,0:T(8,128)(2,1)} %bitcast.9, bf16[2,3,3,128,512]{4,3,2,1,0:T(8,128)(2,1)} %bitcast.8, bf16[3,4,256,512]{3,2,1,0:T(8,128)(2,1)} %bitcast.7), custom_call_target="tpu_custom_call" | custom-call | tf_op jit(solution)/shard_map/pallas_call | solution.py:390
  47.5 1.8 %shard_map.51 = (bf16[4,256,512]{2,1,0:T(8,128)(2,1)}, f32[2,576,512]{2,1,0:T(8,128)}) custom-call(bf16[4,256,512]{2,1,0:T(8,128)(2,1)S(1)} %get-tuple-element.6.final_ref, f32[2,576,512]{2,1,0:T(8,128)S(1)} %get-tuple-element.7.grads_ref), custom_call_target="tpu_custom_call" | custom-call | tf_op jit(solution)/shard_map/pallas_call | solution.py:419

commit v4 on v3

--- a/solution.py
+++ b/solution.py
@@ -40,6 +40,7 @@
     gsend,
     gown,
     grecv,
+    first_sem,
     in_sem,
     send_sem,
     weight_sem,
@@ -66,7 +67,7 @@
 
     def first_copy(group):
         return pltpu.make_async_copy(
-            states_ref.at[:, :, lanes(group)], inbuf.at[0, group], in_sem.at[0, group, 0]
+            states_ref.at[:, :, lanes(group)], inbuf.at[0, group], first_sem.at[group]
         )
 
     def feed_copies(tick, group):
@@ -74,7 +75,7 @@
             yield pltpu.make_async_copy(
                 feed_ref.at[tick - 1, pl.ds(first, size), :, lanes(group)],
                 inbuf.at[tick, group, pl.ds(first, size)],
-                in_sem.at[tick, group, part],
+                in_sem.at[tick - 1, group, part],
             )
 
     def weight_copy(group, branch, column):
@@ -82,26 +83,26 @@
         return pltpu.make_async_copy(
             kernels_ref.at[branch, :, column, :, lanes(group)],
             weights.at[branch, group, pl.ds(row, 3), :, pl.ds(place * GW, GW)],
-            weight_sem.at[branch, group],
-        )
-
-    def weights_arrived(group, branch):
-        whole = kernels_ref.at[branch, :, :, :, lanes(group)]
-        pltpu.make_async_copy(whole, whole, weight_sem.at[branch, group]).wait()
+            weight_sem.at[group],
+        )
+
+    def weights_arrived(group):
+        whole = kernels_ref.at[:, :, :, :, lanes(group)]
+        pltpu.make_async_copy(whole, whole, weight_sem.at[group]).wait()
 
     def below_copy(tick, group, first, size, part):
         return pltpu.make_async_remote_copy(
             src_ref=outbuf.at[tick, group, pl.ds(first, size)],
             dst_ref=inbuf.at[tick + 1, group, pl.ds(first, size)],
-            send_sem=send_sem.at[part],
-            recv_sem=in_sem.at[tick + 1, group, part],
+            send_sem=send_sem.at[0],
+            recv_sem=in_sem.at[tick, group, part],
             device_id={"section": me - 1},
             device_id_type=MESH,
         )
 
     def arrived(tick, group, part):
         pair = inbuf.at[tick, group, pl.ds(1, 2)]
-        pltpu.make_async_copy(pair, pair, in_sem.at[tick, group, part]).wait()
+        pltpu.make_async_copy(pair, pair, in_sem.at[tick - 1, group, part]).wait()
 
     def share_copy(group, branch, offset):
         partner = lax.rem(mine + offset, shards)
@@ -109,7 +110,7 @@
             src_ref=gsend.at[branch, group, pl.ds(pl.multiple_of(partner * share, 16), share)],
             dst_ref=grecv.at[offset - 1, branch, group],
             send_sem=gsend_sem.at[offset - 1, branch],
-            recv_sem=grecv_sem.at[offset - 1, branch, group],
+            recv_sem=grecv_sem.at[offset - 1, group],
             device_id={"dp": partner},
             device_id_type=MESH,
         )
@@ -251,7 +252,7 @@
 
         if first:
             first_copy(group).wait()
-            weights_arrived(group, 1)
+            weights_arrived(group)
         else:
             arrived(tick, group, 0)
         one = stream(0)
@@ -280,7 +281,6 @@
         keep(2, total_one)
         if first:
             give((2, 1, 1))
-            weights_arrived(group, 0)
             prepare(0, group)
         wide_two = input_two.astype(jnp.float32)
         act_two = jax.nn.silu(wide_two).astype(jnp.bfloat16)
@@ -347,10 +347,12 @@
 
     @pl.loop(0, groups)
     def _(group):
+        for offset in range(1, shards):
+            both = grecv.at[offset - 1, :, group]
+            pltpu.make_async_copy(both, both, grecv_sem.at[offset - 1, group]).wait()
         for branch in (1, 0):
             total = gown[branch, group, pl.ds(pl.multiple_of(mine * share, 16), share), :]
             for offset in range(1, shards):
-                share_copy(group, branch, offset).wait_recv()
                 total = total + grecv[offset - 1, branch, group].astype(jnp.float32)
             grads_ref[branch, :, lanes(group)] = total
 
@@ -358,9 +360,8 @@
 
     @pl.when(has_below)
     def _():
-        for part in range(2):
-            every = outbuf.at[pl.ds(0, ticks - 1), :, pl.ds(0, 2)]
-            pltpu.make_async_copy(every, every, send_sem.at[part]).wait()
+        every = outbuf.at[pl.ds(0, ticks - 1)]
+        pltpu.make_async_copy(every, every, send_sem.at[0]).wait()
 
 
 def write_kernel(final_ref, grads_ref, final_out, grads_out, sems):
@@ -405,12 +406,13 @@
             pltpu.VMEM((2, groups, taps_rows, GW), jnp.bfloat16),
             pltpu.VMEM((2, groups, taps_rows, GW), jnp.float32),
             pltpu.VMEM((max(shards - 1, 1), 2, groups, share, GW), jnp.bfloat16),
-            dma((ticks, groups, 2)),
-            dma((2,)),
-            dma((2, groups)),
+            dma((groups,)),
+            dma((ticks - 1, groups, 2)),
+            dma((1,)),
+            dma((groups,)),
             pltpu.SemaphoreType.REGULAR,
             dma((max(shards - 1, 1), 2)),
-            dma((max(shards - 1, 1), 2, groups)),
+            dma((max(shards - 1, 1), groups)),
         ],
         compiler_params=pltpu.CompilerParams(
             collective_id=0, has_side_effects=True, vmem_limit_bytes=56 * 1024 * 1024

time: 49.6 us -> 49.7 us (level)
  no operation moved by 1% of the time
where the time goes in v4:
time: 49.7 us; the launch traced here: 49.3 us
  Pallas kernels  48.6 us (98%)
  between operations  0.64 us (1%)
    pallas_call x1, Pallas kernels, on_device(): pl.pallas_call(functools.partial(fused_kernel, dims), out_shape=(pltpu.VM...  46.9 us
    pallas_call x1, Pallas kernels, on_device(): pl.pallas_call(write_kernel, out_shape=(jax.ShapeDtypeStruct(final.shape,...  1.77 us

profile of v4, /device:TPU:0, one launch (start us, length us, event | category | flops | bytes accessed | tf_op | source)
XLA Modules:
  0.0 49.3 jit_solution(7093020769990262389)
XLA Ops:
  0.6 46.9 %shard_map.50 = (bf16[4,256,512]{2,1,0:T(8,128)(2,1)S(1)}, f32[2,576,512]{2,1,0:T(8,128)S(1)}) custom-call(bf16[4,256,512]{2,1,0:T(8,128)(2,1)} %bitcast.9, bf16[2,3,3,128,512]{4,3,2,1,0:T(8,128)(2,1)} %bitcast.8, bf16[3,4,256,512]{3,2,1,0:T(8,128)(2,1)} %bitcast.7), custom_call_target="tpu_custom_call" | custom-call | tf_op jit(solution)/shard_map/pallas_call | solution.py:391
  47.5 1.8 %shard_map.51 = (bf16[4,256,512]{2,1,0:T(8,128)(2,1)}, f32[2,576,512]{2,1,0:T(8,128)}) custom-call(bf16[4,256,512]{2,1,0:T(8,128)(2,1)S(1)} %get-tuple-element.6.final_ref, f32[2,576,512]{2,1,0:T(8,128)S(1)} %get-tuple-element.7.grads_ref), custom_call_target="tpu_custom_call" | custom-call | tf_op jit(solution)/shard_map/pallas_call | solution.py:421

commit v5 on v4

--- a/solution.py
+++ b/solution.py
@@ -289,16 +289,18 @@
         if last:
             hand_on(0, group, act_two, 3)
         keep(0, (stream(0) - mix(2, weights[0, group])).astype(jnp.bfloat16))
+        if not last:
+            give((0, 1, 0))
         keep(
             3,
             (stream(3) + mix(3, flipped[0, group]) * smooth_grad(wide_two)).astype(jnp.bfloat16),
         )
         if first:
-            give((0, 1, 0), (3, 1, 0))
+            give((3, 1, 0))
             acc[1, group] = term_of(act_one, 1)
             acc[0, group] = term_of(act_two, 3)
         elif not last:
-            give((0, 1, 0), (3, 1, 0), (1, 2, 1))
+            give((3, 1, 0), (1, 2, 1))
             acc[1, group] += term_of(act_one, 1)
             acc[0, group] += term_of(act_two, 3)
 

time: 49.7 us -> 49.7 us (level)
  no operation moved by 1% of the time
where the time goes in v5:
time: 49.7 us; the launch traced here: 49.3 us
  Pallas kernels  48.7 us (98%)
  between operations  0.64 us (1%)
    pallas_call x1, Pallas kernels, on_device(): pl.pallas_call(functools.partial(fused_kernel, dims), out_shape=(pltpu.VM...  46.9 us
    pallas_call x1, Pallas kernels, on_device(): pl.pallas_call(write_kernel, out_shape=(jax.ShapeDtypeStruct(final.shape,...  1.77 us

profile of v5, /device:TPU:0, one launch (start us, length us, event | category | flops | bytes accessed | tf_op | source)
XLA Modules:
  0.0 49.3 jit_solution(9686811367141767900)
XLA Ops:
  0.6 46.9 %shard_map.50 = (bf16[4,256,512]{2,1,0:T(8,128)(2,1)S(1)}, f32[2,576,512]{2,1,0:T(8,128)S(1)}) custom-call(bf16[4,256,512]{2,1,0:T(8,128)(2,1)} %bitcast.9, bf16[2,3,3,128,512]{4,3,2,1,0:T(8,128)(2,1)} %bitcast.8, bf16[3,4,256,512]{3,2,1,0:T(8,128)(2,1)} %bitcast.7), custom_call_target="tpu_custom_call" | custom-call | tf_op jit(solution)/shard_map/pallas_call | solution.py:393
  47.6 1.8 %shard_map.51 = (bf16[4,256,512]{2,1,0:T(8,128)(2,1)}, f32[2,576,512]{2,1,0:T(8,128)}) custom-call(bf16[4,256,512]{2,1,0:T(8,128)(2,1)S(1)} %get-tuple-element.6.final_ref, f32[2,576,512]{2,1,0:T(8,128)S(1)} %get-tuple-element.7.grads_ref), custom_call_target="tpu_custom_call" | custom-call | tf_op jit(solution)/shard_map/pallas_call | solution.py:423

commit v6 on v4

--- a/solution.py
+++ b/solution.py
@@ -57,8 +57,8 @@
     count = lax.axis_size("section")
     mine = lax.axis_index("dp")
     is_top = me == count - 1
-    lower = jnp.logical_and(lax.rem(me, 2) == 0, me < count - 1)
-    upper = lax.rem(me, 2) == 1
+    lower = jnp.logical_and(me == 0, me < count - 1)
+    upper = me == 1
     has_below = me > 0
 
     def lanes(group):
@@ -219,7 +219,7 @@
             gsend[branch, group, k * GW : (k + 1) * GW, :] = block.astype(jnp.bfloat16)
         waiting = branch == 0 and shards > 1
 
-        @pl.when(jnp.logical_or(not waiting, jnp.logical_or(lax.rem(me, 2) == 0, group < groups - 1)))
+        @pl.when(jnp.logical_or(not waiting, jnp.logical_or(me != 1, group < groups - 1)))
         def _():
             for offset in range(1, shards):
                 share_copy(group, branch, offset).start()

time: 49.7 us -> 49.7 us (level)
  no operation moved by 1% of the time
where the time goes in v6:
time: 49.7 us; the launch traced here: 49.3 us
  Pallas kernels  48.7 us (98%)
  between operations  0.64 us (1%)
    pallas_call x1, Pallas kernels, on_device(): pl.pallas_call(functools.partial(fused_kernel, dims), out_shape=(pltpu.VM...  46.9 us
    pallas_call x1, Pallas kernels, on_device(): pl.pallas_call(write_kernel, out_shape=(jax.ShapeDtypeStruct(final.shape,...  1.77 us

profile of v6, /device:TPU:0, one launch (start us, length us, event | category | flops | bytes accessed | tf_op | source)
XLA Modules:
  0.0 49.3 jit_solution(10972280222676567932)
XLA Ops:
  0.6 46.9 %shard_map.50 = (bf16[4,256,512]{2,1,0:T(8,128)(2,1)S(1)}, f32[2,576,512]{2,1,0:T(8,128)S(1)}) custom-call(bf16[4,256,512]{2,1,0:T(8,128)(2,1)} %bitcast.9, bf16[2,3,3,128,512]{4,3,2,1,0:T(8,128)(2,1)} %bitcast.8, bf16[3,4,256,512]{3,2,1,0:T(8,128)(2,1)} %bitcast.7), custom_call_target="tpu_custom_call" | custom-call | tf_op jit(solution)/shard_map/pallas_call | solution.py:391
  47.5 1.8 %shard_map.51 = (bf16[4,256,512]{2,1,0:T(8,128)(2,1)}, f32[2,576,512]{2,1,0:T(8,128)}) custom-call(bf16[4,256,512]{2,1,0:T(8,128)(2,1)S(1)} %get-tuple-element.6.final_ref, f32[2,576,512]{2,1,0:T(8,128)S(1)} %get-tuple-element.7.grads_ref), custom_call_target="tpu_custom_call" | custom-call | tf_op jit(solution)/shard_map/pallas_call | solution.py:421

commit v7 on v4

--- a/solution.py
+++ b/solution.py
@@ -18,7 +18,7 @@
 
 
 def steps_in_order(groups, ticks):
-    tuned = ((0, 0), (0, 1), (1, 0), (0, 2), (1, 1), (0, 3), (2, 0), (1, 2), (2, 1), (1, 3), (3, 0), (2, 2), (3, 1), (2, 3), (3, 2), (3, 3))
+    tuned = ((0, 0), (0, 1), (1, 0), (0, 2), (1, 1), (2, 0), (0, 3), (1, 2), (2, 1), (1, 3), (3, 0), (2, 2), (3, 1), (2, 3), (3, 2), (3, 3))
     if sorted(tuned) == [(group, tick) for group in range(groups) for tick in range(ticks)]:
         return tuned
     return [(group, tick) for tick in range(ticks) for group in range(groups)]

time: 49.7 us -> 49.7 us (level)
  no operation moved by 1% of the time
where the time goes in v7:
time: 49.7 us; the launch traced here: 49.3 us
  Pallas kernels  48.6 us (98%)
  between operations  0.64 us (1%)
    pallas_call x1, Pallas kernels, on_device(): pl.pallas_call(functools.partial(fused_kernel, dims), out_shape=(pltpu.VM...  46.9 us
    pallas_call x1, Pallas kernels, on_device(): pl.pallas_call(write_kernel, out_shape=(jax.ShapeDtypeStruct(final.shape,...  1.77 us

profile of v7, /device:TPU:0, one launch (start us, length us, event | category | flops | bytes accessed | tf_op | source)
XLA Modules:
  0.0 49.3 jit_solution(6350822933911509291)
XLA Ops:
  0.6 46.9 %shard_map.50 = (bf16[4,256,512]{2,1,0:T(8,128)(2,1)S(1)}, f32[2,576,512]{2,1,0:T(8,128)S(1)}) custom-call(bf16[4,256,512]{2,1,0:T(8,128)(2,1)} %bitcast.9, bf16[2,3,3,128,512]{4,3,2,1,0:T(8,128)(2,1)} %bitcast.8, bf16[3,4,256,512]{3,2,1,0:T(8,128)(2,1)} %bitcast.7), custom_call_target="tpu_custom_call" | custom-call | tf_op jit(solution)/shard_map/pallas_call | solution.py:391
  47.5 1.8 %shard_map.51 = (bf16[4,256,512]{2,1,0:T(8,128)(2,1)}, f32[2,576,512]{2,1,0:T(8,128)}) custom-call(bf16[4,256,512]{2,1,0:T(8,128)(2,1)S(1)} %get-tuple-element.6.final_ref, f32[2,576,512]{2,1,0:T(8,128)S(1)} %get-tuple-element.7.grads_ref), custom_call_target="tpu_custom_call" | custom-call | tf_op jit(solution)/shard_map/pallas_call | solution.py:421
